TPU v7x, 32 devices: a whole 2x2x4 slice. The times are simulated.
32 devices in a mesh: layer: 2 (over y), neuron: 4 (over z), token: 4 (over x, core).
Axes of the slice: x: 2, y: 2, z: 4, core: 2. Of those that a mesh axis runs over, the one named last changes fastest.
Arguments:
- tokens: bfloat16 [4096, 8192], P(('layer', 'token'), 'neuron'), parts along dimension 0, may hold values from -6 to 6
- up_weight: bfloat16 [16384, 14336], P(('layer', 'token'), 'neuron'), parts along dimension 0, may hold values from -0.0625 to 0.0625
- encoder: bfloat16 [16384, 1024], P(('layer', 'token'), 'neuron'), parts along dimension 0, may hold values from -0.0625 to 0.0625
- decoder: bfloat16 [2048, 14336], P(('layer', 'token'), 'neuron'), parts along dimension 0, may hold values from -0.1875 to 0.1875
Outputs:
- grad_encoder: float32 [16384, 1024], P(('layer', 'token'), 'neuron'), parts along dimension 0
- grad_decoder: float32 [2048, 14336], P(('layer', 'token'), 'neuron'), parts along dimension 0
There are 2 independent parts, one for each index of `layer`. A program takes and returns all parts, laid end to end along the dimension named above; each array names one. Nothing has to cross between parts.
All inputs are finite; a program needn't handle non-finite values.
Results may differ from a plain program's by a relative error of at most 0.0034.
Values may be sent and summed in bfloat16 or wider, within the bound.
No kernel may reach another device: no remote copies, remote signals or barrier semaphores. Data moves between devices by JAX's collectives and lax.ppermute only.
A program may use at most 128 MiB of HBM per device.

v0:
```python
import math

import jax
import jax.numpy as jnp
from jax import lax
from jax.experimental import pallas as pl
from jax.experimental.pallas import tpu as pltpu
from jax.sharding import PartitionSpec as P


SHARES = (6, 10, 10, 6)
CHUNKS = len(SHARES)
F32 = jnp.float32
BF16 = jnp.bfloat16


def dot(left, right, dims=((1,), (0,))):
    return lax.dot_general(left, right, (dims, ((), ())), preferred_element_type=F32)


def block(array, start, size, axis):
    starts = [start if d == axis else 0 for d in range(array.ndim)]
    sizes = [size if d == axis else n for d, n in enumerate(array.shape)]
    return lax.dynamic_slice(array, starts, sizes, allow_negative_indices=False)


def blocks_kernel(order_ref, left_ref, right_ref, out_ref):
    rows = left_ref.shape[0]
    step = rows // 4 if rows % 64 == 0 else rows
    for start in range(0, rows, step):
        at = pl.ds(start, step)
        out_ref[0, at, :] = jnp.dot(
            left_ref[at, :], right_ref[...], preferred_element_type=F32
        ).astype(BF16)


def column_blocks(left, right, order, columns):
    rows, depth = left.shape
    count = order.shape[0]
    return pl.pallas_call(
        blocks_kernel,
        grid_spec=pltpu.PrefetchScalarGridSpec(
            num_scalar_prefetch=1,
            grid=(count,),
            in_specs=[
                pl.BlockSpec((rows, depth), lambda j, order: (0, 0)),
                pl.BlockSpec((depth, columns), lambda j, order: (0, order[j])),
            ],
            out_specs=pl.BlockSpec((1, rows, columns), lambda j, order: (j, 0, 0)),
        ),
        out_shape=jax.ShapeDtypeStruct((count, rows, columns), BF16),
        compiler_params=pltpu.CompilerParams(vmem_limit_bytes=32 << 20),
        cost_estimate=pl.CostEstimate(
            flops=2 * rows * depth * columns * count,
            bytes_accessed=2 * (rows * depth + (depth + rows) * columns * count),
            transcendentals=0,
        ),
    )(order, left, pltpu.with_memory_space_constraint(right, pltpu.HBM))


def per_device(tokens, up_weight, encoder, decoder):
    row_count, width = tokens.shape
    tokens_on, neurons_on = lax.axis_size("token"), lax.axis_size("neuron")
    cores = 2 if tokens_on % 2 == 0 else 1
    chips = tokens_on // cores
    total_rows = row_count * tokens_on
    me = lax.axis_index("token")
    plane = lax.axis_index("neuron")
    chip, core = lax.div(me, cores), lax.rem(me, cores)
    columns = up_weight.shape[1] // tokens_on
    ranks = encoder.shape[1]
    edges = [row_count * sum(SHARES[:k]) // sum(SHARES) for k in range(len(SHARES) + 1)]

    def swap(array):
        return lax.ppermute(array, "token", [(i, i ^ 1) for i in range(tokens_on)])

    def across(array, step):
        return lax.ppermute(
            array,
            "token",
            [(i, (i // cores + step) % chips * cores + i % cores) for i in range(tokens_on)],
        )

    def exchange(array, step, other):
        pairs = [
            (i, (i // cores + step) % chips * cores + (i % cores ^ other))
            for i in range(tokens_on)
        ]
        return lax.ppermute(array, "token", pairs)

    def upward(array, step):
        return lax.ppermute(
            array, "neuron", [(i, (i + step) % neurons_on) for i in range(neurons_on)]
        )

    def gathered_of(k):
        rows = tokens[edges[k] : edges[k + 1]]
        if neurons_on % tokens_on == 0:
            return lax.all_gather(rows, "neuron", axis=0)
        return lax.all_gather(rows, "neuron", axis=1, tiled=True)

    def spread_of(gathered):
        if neurons_on % tokens_on:
            return lax.all_to_all(
                gathered, "token", split_axis=1, concat_axis=0, tiled=True
            )
        moved = lax.all_to_all(gathered, "token", split_axis=0, concat_axis=0, tiled=True)
        ratio = neurons_on // tokens_on
        if ratio == 1:
            return moved.reshape(-1, width)
        moved = moved.reshape(tokens_on, ratio, -1, width)
        return moved.transpose(0, 2, 1, 3).reshape(-1, ratio * width)

    def half(array, index, axis):
        size = array.shape[axis] // cores
        parts = [lax.slice_in_dim(array, j * size, (j + 1) * size, axis=axis) for j in range(cores)]
        return parts[0] if cores == 1 else jnp.where(index == 0, *parts)

    def both_halves(mine):
        if cores == 1:
            return mine
        theirs = swap(mine)
        first = jnp.where(core == 0, mine, theirs)
        second = jnp.where(core == 0, theirs, mine)
        return jnp.concatenate([first, second], axis=0)

    def partials_of(piece):
        steps = list(range(1, chips)) + [0]
        order = [
            lax.rem(chip + step, chips) * cores + (core ^ other)
            for other in reversed(range(cores))
            for step in steps
        ]
        if columns % 128:
            terms = [
                dot(piece, block(up_weight, at * columns, columns, 1)).astype(BF16)
                for at in order
            ]
            return jnp.stack(terms).reshape(cores, chips, -1, columns)
        terms = column_blocks(piece, up_weight, jnp.stack(order), columns)
        return terms.reshape(cores, chips, -1, columns)

    def labels_of(piece):
        terms = partials_of(piece)
        kept = terms[cores - 1]
        if cores == 2:
            moved = swap(terms[0])
            kept = [kept[j].astype(F32) + moved[j].astype(F32) for j in range(chips)]
        total = kept[chips - 1]
        for step in range(1, chips):
            moved = across(kept[step - 1].astype(BF16), step)
            total = total + moved.astype(F32)
        return total

    def hidden_of(piece):
        terms = dot(piece, encoder)
        summed = half(terms, core, 0)
        if cores == 2:
            sent = half(terms, 1 - core, 0)
            sent = swap(sent)
            summed = summed + sent
        whole = summed
        for step in range(1, chips):
            moved = across(summed, step)
            whole = whole + moved
        shared = [whole.astype(BF16)]
        for step in range(1, neurons_on):
            shared.append(upward(shared[0], step))
        wide = [
            lax.select_n(lax.rem(plane + neurons_on - j, neurons_on), *shared)
            for j in range(neurons_on)
        ]
        return both_halves(jnp.concatenate(wide, axis=1))

    def back_of(scaled, decoder_own):
        terms = dot(scaled, decoder_own, ((1,), (1,)))
        summed = half(terms, core, 0)
        if cores == 2:
            sent = half(terms, 1 - core, 0).astype(BF16)
            sent = swap(sent)
            summed = summed + sent.astype(F32)
        parts = [
            lax.slice_in_dim(summed, j * ranks, (j + 1) * ranks, axis=1)
            for j in range(neurons_on)
        ]
        own = lax.select_n(plane, *parts)
        for step in range(1, neurons_on):
            sent = lax.select_n(lax.rem(plane + step, neurons_on), *parts).astype(BF16)
            moved = upward(sent, step)
            own = own + moved.astype(F32)
        whole = own
        for step in range(1, chips):
            sent = own.astype(BF16)
            moved = across(sent, step)
            whole = whole + moved.astype(F32)
        return both_halves(whole.astype(BF16))

    gathered = [gathered_of(k) for k in range(CHUNKS)]
    arrived = []
    for step in range(chips):
        for other in range(cores):
            there = lax.rem(chip + step, chips) * cores + (core ^ other)
            sent = block(decoder, there * columns, columns, 1)
            if step or other:
                sent = exchange(sent, step, other)
            arrived.append(sent)
    decoder_own = []
    for j in range(tokens_on):
        which = lax.rem(chip + chips - j // cores, chips) * cores + (core ^ (j % cores))
        decoder_own.append(lax.select_n(which, *arrived))
    decoder_own = jnp.concatenate(decoder_own, axis=0)
    grad_encoder, grad_decoder = None, None
    for k in range(CHUNKS):
        piece = spread_of(gathered[k])
        labels = jax.nn.relu(labels_of(piece))
        hidden = hidden_of(piece)
        predicted = dot(hidden, decoder_own)
        scaled = ((predicted - labels) / math.sqrt(total_rows)).astype(BF16)
        term = dot(hidden, scaled, ((0,), (0,)))
        grad_decoder = term if grad_decoder is None else lax.optimization_barrier(grad_decoder) + term
        back = back_of(scaled, decoder_own)
        term = dot(piece, back, ((0,), (0,)))
        grad_encoder = term if grad_encoder is None else lax.optimization_barrier(grad_encoder) + term
    grad_decoder = lax.all_to_all(
        grad_decoder.astype(BF16).reshape(tokens_on, -1, columns),
        "token",
        split_axis=0,
        concat_axis=0,
        tiled=True,
    )
    grad_decoder = jnp.concatenate([grad_decoder[j] for j in range(tokens_on)], axis=1)
    return (grad_encoder, grad_decoder.astype(F32))


def solution(mesh):
    return jax.shard_map(
        per_device,
        mesh=mesh,
        in_specs=(P(("layer", "token"), "neuron"),) * 4,
        out_specs=(P(("layer", "token"), "neuron"),) * 2,
        check_vma=False,
    )
```

profile of v0, /device:TPU:0, one launch (start us, length us, event | category | flops | bytes accessed | tf_op | source)
XLA Modules:
  0.0 472.6 jit_solution(3065633614610271271)
XLA Ops:
  12.7 37.2 %all-gather.9.cloned.1.call-done = bf16[384,2048]{1,0:T(8,128)(2,1)} async-done(((bf16[96,2048]{1,0:T(8,128)(2,1)}), bf16[384,2048]{1,0:T(8,128)(2,1)}) %all-gather.9.cloned.1.call-update) | async-done | bytes 1572880 | tf_op jit(solution)/shard_map/all_gather | solution.py:99
  58.1 29.9 %all-gather.15.cloned.1.call-done = bf16[384,2048]{1,0:T(8,128)(2,1)} async-done(((bf16[96,2048]{1,0:T(8,128)(2,1)}), bf16[384,2048]{1,0:T(8,128)(2,1)}) %all-gather.15.cloned.1.call-update) | async-done | bytes 1572880 | tf_op jit(solution)/shard_map/all_gather | solution.py:99
  96.6 12.7 %shard_map.59 = bf16[4,384,896]{2,1,0:T(8,128)(2,1)S(1)} custom-call(s32[4]{0:T(128)S(1)} %pad_add_fusion.order_ref, bf16[384,2048]{1,0:T(8,128)(2,1)S(1)} %bitcast.101, bf16[2048,3584]{1,0:T(8,128)(2,1)} %right_ref.7), custom_call_target="tpu_custom_call" | custom-call | flops 5637144576 | bytes 19005440 | tf_op jit(solution)/shard_map/pallas_call | solution.py:40
  112.7 12.7 %shard_map.62 = bf16[4,384,896]{2,1,0:T(8,128)(2,1)S(1)} custom-call(s32[4]{0:T(128)S(1)} %pad_add_fusion.order_ref, bf16[384,2048]{1,0:T(8,128)(2,1)S(1)} %bitcast.97, bf16[2048,3584]{1,0:T(8,128)(2,1)} %right_ref.7), custom_call_target="tpu_custom_call" | custom-call | flops 5637144576 | bytes 19005440 | tf_op jit(solution)/shard_map/pallas_call | solution.py:40
  135.8 5.1 %collective-permute-done.1 = f32[192,256]{1,0:T(8,128)S(1)} collective-permute-done((f32[192,256]{1,0:T(8,128)S(1)}, f32[192,256]{1,0:T(8,128)S(1)}, u32[]{:S(2)}, u32[]{:S(2)}) %collective-permute-start.1) | collective-permute-done | bytes 196640 | tf_op jit(solution)/shard_map/ppermute | solution.py:78
  143.9 4.5 all-to-all-start.1
  156.4 11.0 %collective-permute-done.48 = bf16[192,256]{1,0:T(8,128)(2,1)S(1)} collective-permute-done((bf16[192,256]{1,0:T(8,128)(2,1)S(1)}, bf16[192,256]{1,0:T(8,128)(2,1)S(1)}, u32[]{:S(2)}, u32[]{:S(2)}) %collective-permute-start.48) | collective-permute-done | bytes 98336 | tf_op jit(solution)/shard_map/ppermute | solution.py:92
  174.4 20.7 %collective-permute-done.10 = bf16[384,896]{1,0:T(8,128)(2,1)S(1)} collective-permute-done((bf16[384,896]{1,0:T(8,128)(2,1)S(1)}, bf16[384,896]{1,0:T(8,128)(2,1)S(1)}, u32[]{:S(2)}, u32[]{:S(2)}) %collective-permute-start.10) | collective-permute-done | bytes 688160 | tf_op jit(solution)/shard_map/ppermute | solution.py:78
  200.3 8.9 %collective-permute-done.52 = bf16[384,896]{1,0:T(8,128)(2,1)S(1)} collective-permute-done((bf16[384,896]{1,0:T(8,128)(2,1)S(1)}, bf16[384,896]{1,0:T(8,128)(2,1)S(1)}, u32[]{:S(2)}, u32[]{:S(2)}) %collective-permute-start.52) | collective-permute-done | bytes 688160 | tf_op jit(solution)/shard_map/ppermute | solution.py:78
  214.4 4.5 all-to-all-start.2
  221.6 4.2 fusion.23
  231.4 15.1 %shard_map.60 = bf16[4,640,896]{2,1,0:T(8,128)(2,1)S(1)} custom-call(s32[4]{0:T(128)S(1)} %pad_add_fusion.order_ref, bf16[640,2048]{1,0:T(8,128)(2,1)} %bitcast.10.left_ref, bf16[2048,3584]{1,0:T(8,128)(2,1)} %right_ref.7), custom_call_target="tpu_custom_call" | custom-call | flops 9395240960 | bytes 21889024 | tf_op jit(solution)/shard_map/pallas_call | solution.py:40
  250.3 15.1 %shard_map.61 = bf16[4,640,896]{2,1,0:T(8,128)(2,1)S(1)} custom-call(s32[4]{0:T(128)S(1)} %pad_add_fusion.order_ref, bf16[640,2048]{1,0:T(8,128)(2,1)} %bitcast.15.left_ref, bf16[2048,3584]{1,0:T(8,128)(2,1)} %right_ref.7), custom_call_target="tpu_custom_call" | custom-call | flops 9395240960 | bytes 21889024 | tf_op jit(solution)/shard_map/pallas_call | solution.py:40
  292.0 4.7 %collective-permute-done.15 = bf16[192,256]{1,0:T(8,128)(2,1)S(1)} collective-permute-done((bf16[192,256]{1,0:T(8,128)(2,1)S(1)}, bf16[192,256]{1,0:T(8,128)(2,1)S(1)}, u32[]{:S(2)}, u32[]{:S(2)}) %collective-permute-start.15) | collective-permute-done | bytes 98336 | tf_op jit(solution)/shard_map/ppermute | solution.py:78
  297.1 4.2 collective-permute-done.57
  303.7 8.4 %collective-permute-done.18 = f32[320,256]{1,0:T(8,128)S(1)} collective-permute-done((f32[320,256]{1,0:T(8,128)S(1)}, f32[320,256]{1,0:T(8,128)S(1)}, u32[]{:S(2)}, u32[]{:S(2)}) %collective-permute-start.18) | collective-permute-done | bytes 327712 | tf_op jit(solution)/shard_map/ppermute | solution.py:78
  329.3 6.7 %collective-permute-start.33 = (bf16[320,256]{1,0:T(8,128)(2,1)S(1)}, bf16[320,256]{1,0:T(8,128)(2,1)S(1)}, u32[]{:S(2)}, u32[]{:S(2)}) collective-permute-start(bf16[320,256]{1,0:T(8,128)(2,1)S(1)} %add_convert_fusion.6), channel_id=1, source_target_pairs={{0,4},{4,8},{8,12},{12,0},{1,5},{5,9},{9,13},{13,1},{2,6},{6,10},{... | collective-permute-start | bytes 491528 | tf_op jit(solution)/shard_map/ppermute | solution.py:92
  336.3 5.6 %collective-permute-done.35 = bf16[320,256]{1,0:T(8,128)(2,1)S(1)} collective-permute-done((bf16[320,256]{1,0:T(8,128)(2,1)S(1)}, bf16[320,256]{1,0:T(8,128)(2,1)S(1)}, u32[]{:S(2)}, u32[]{:S(2)}) %collective-permute-start.35) | collective-permute-done | bytes 163872 | tf_op jit(solution)/shard_map/ppermute | solution.py:92
  348.2 23.0 %collective-permute-done.24 = bf16[640,896]{1,0:T(8,128)(2,1)S(1)} collective-permute-done((bf16[640,896]{1,0:T(8,128)(2,1)S(1)}, bf16[640,896]{1,0:T(8,128)(2,1)S(1)}, u32[]{:S(2)}, u32[]{:S(2)}) %collective-permute-start.24) | collective-permute-done | bytes 1146912 | tf_op jit(solution)/shard_map/ppermute | solution.py:78
  377.3 17.5 %collective-permute-done.38 = bf16[640,896]{1,0:T(8,128)(2,1)S(1)} collective-permute-done((bf16[640,896]{1,0:T(8,128)(2,1)S(1)}, bf16[640,896]{1,0:T(8,128)(2,1)S(1)}, u32[]{:S(2)}, u32[]{:S(2)}) %collective-permute-start.38) | collective-permute-done | bytes 1146912 | tf_op jit(solution)/shard_map/ppermute | solution.py:78
  405.5 4.6 all-to-all-start.4
  420.0 7.6 %collective-permute-start.40 = (bf16[320,256]{1,0:T(8,128)(2,1)S(1)}, bf16[320,256]{1,0:T(8,128)(2,1)S(1)}, u32[]{:S(2)}, u32[]{:S(2)}) collective-permute-start(bf16[320,256]{1,0:T(8,128)(2,1)S(1)} %get-tuple-element.27), channel_id=1, source_target_pairs={{0,4},{4,8},{8,12},{12,0},{1,5},{5,9},{9,13},{13,1},{2,6},{6,10},{... | collective-permute-start | bytes 491528 | tf_op jit(solution)/shard_map/ppermute | solution.py:92
  431.5 8.7 %collective-permute-start.29 = (bf16[320,256]{1,0:T(8,128)(2,1)S(1)}, bf16[320,256]{1,0:T(8,128)(2,1)S(1)}, u32[]{:S(2)}, u32[]{:S(2)}) collective-permute-start(bf16[320,256]{1,0:T(8,128)(2,1)S(1)} %get-tuple-element.8), channel_id=1, source_target_pairs={{0,2},{1,3},{2,0},{3,1},{4,6},{5,7},{6,4},{7,5},{8,10},{9,11},{10,... | collective-permute-start | bytes 491528 | tf_op jit(solution)/shard_map/ppermute | solution.py:78
  440.2 4.4 collective-permute-done.41
  (284 shorter events, 180.1 us)
Async XLA Ops:
  7.2 42.7 %all-gather.9.cloned.1.call-start = ((), (), s32[]{:S(2)}) async-start(), calls=%async_computation.5 | async-start | bytes 1966080 | tf_op jit(solution)/shard_map/all_gather | solution.py:99
  9.4 78.6 %all-gather.15.cloned.1.call-start = ((), (), s32[]{:S(2)}) async-start(), calls=%async_computation.8 | async-start | bytes 1966080 | tf_op jit(solution)/shard_map/all_gather | solution.py:99
  10.2 133.8 %all-gather.11.cloned.1.call-start = ((), (), s32[]{:S(2)}) async-start(), calls=%async_computation.6 | async-start | bytes 3276800 | tf_op jit(solution)/shard_map/all_gather | solution.py:99
  49.9 38.1 %all-to-all-start = ((bf16[4,96,2048]{2,1,0:T(8,128)(2,1)}), bf16[4,96,2048]{2,1,0:T(8,128)(2,1)S(1)}, u32[]{:S(2)}, u32[]{:S(2)}) async-start(bf16[4,96,2048]{2,1,0:T(8,128)(2,1)} %bitcast.107), calls=%async_computation | async-start | bytes 3145728 | tf_op jit(solution)/shard_map/all_to_all | solution.py:107
  53.5 160.9 %all-gather.13.cloned.1.call-start = ((), (), s32[]{:S(2)}) async-start(), calls=%async_computation.7 | async-start | bytes 3276800 | tf_op jit(solution)/shard_map/all_gather | solution.py:99
  55.9 36.9 %collective-permute-start.7 = (bf16[256,896]{1,0:T(8,128)(2,1)}, bf16[256,896]{1,0:T(8,128)(2,1)S(1)}, u32[]{:S(2)}, u32[]{:S(2)}) collective-permute-start(bf16[256,896]{1,0:T(8,128)(2,1)} %get-tuple-element.26), channel_id=1, source_target_pairs={{0,2},{1,3},{2,0},{3,1},{4,6},{5,7},{6,4},{7,5},{8,10},{9,11},{10,... | collective-permute-start | bytes 1376264 | tf_op jit(solution)/shard_map/ppermute | solution.py:89
  57.8 35.0 %collective-permute-start.8 = (bf16[256,896]{1,0:T(8,128)(2,1)}, bf16[256,896]{1,0:T(8,128)(2,1)}, u32[]{:S(2)}, u32[]{:S(2)}) collective-permute-start(bf16[256,896]{1,0:T(8,128)(2,1)} %get-tuple-element.25), channel_id=1, source_target_pairs={{0,3},{1,2},{2,1},{3,0},{4,7},{5,6},{6,5},{7,4},{8,11},{9,10},{10,... | collective-permute-start | bytes 1376264 | tf_op jit(solution)/shard_map/ppermute | solution.py:89
  57.8 35.0 %collective-permute-start.6 = (bf16[256,896]{1,0:T(8,128)(2,1)S(1)}, bf16[256,896]{1,0:T(8,128)(2,1)}, u32[]{:S(2)}, u32[]{:S(2)}) collective-permute-start(bf16[256,896]{1,0:T(8,128)(2,1)S(1)} %get-tuple-element.24), channel_id=1, source_target_pairs={{0,1},{1,0},{2,3},{3,2},{4,5},{5,4},{6,7},{7,6},{8,9},{9,8},{10,11... | collective-permute-start | bytes 1376264 | tf_op jit(solution)/shard_map/ppermute | solution.py:89
  129.4 38.7 %collective-permute-start.9 = (bf16[2,384,896]{2,1,0:T(8,128)(2,1)}, bf16[2,384,896]{2,1,0:T(8,128)(2,1)}, u32[]{:S(2)}, u32[]{:S(2)}) collective-permute-start(bf16[2,384,896]{2,1,0:T(8,128)(2,1)} %slice.283), channel_id=1, source_target_pairs={{0,1},{1,0},{2,3},{3,2},{4,5},{5,4},{6,7},{7,6},{8,9},{9,8},{10,11... | collective-permute-start | bytes 4128776 | tf_op jit(solution)/shard_map/ppermute | solution.py:75
  131.2 40.5 %collective-permute-start.51 = (bf16[2,384,896]{2,1,0:T(8,128)(2,1)}, bf16[2,384,896]{2,1,0:T(8,128)(2,1)}, u32[]{:S(2)}, u32[]{:S(2)}) collective-permute-start(bf16[2,384,896]{2,1,0:T(8,128)(2,1)} %slice.322), channel_id=1, source_target_pairs={{0,1},{1,0},{2,3},{3,2},{4,5},{5,4},{6,7},{7,6},{8,9},{9,8},{10,11... | collective-permute-start | bytes 4128776 | tf_op jit(solution)/shard_map/ppermute | solution.py:75
  143.9 70.4 %all-to-all-start.1 = ((bf16[4,160,2048]{2,1,0:T(8,128)(2,1)}), bf16[4,160,2048]{2,1,0:T(8,128)(2,1)}, u32[]{:S(2)}, u32[]{:S(2)}) async-start(bf16[4,160,2048]{2,1,0:T(8,128)(2,1)} %bitcast.104), calls=%async_computation.1 | async-start | bytes 5242880 | tf_op jit(solution)/shard_map/all_to_all | solution.py:107
  169.4 25.6 %collective-permute-start.10 = (bf16[384,896]{1,0:T(8,128)(2,1)S(1)}, bf16[384,896]{1,0:T(8,128)(2,1)S(1)}, u32[]{:S(2)}, u32[]{:S(2)}) collective-permute-start(bf16[384,896]{1,0:T(8,128)(2,1)S(1)} %fusion.20), channel_id=1, source_target_pairs={{0,2},{1,3},{2,0},{3,1},{4,6},{5,7},{6,4},{7,5},{8,10},{9,11},{10,... | collective-permute-start | bytes 2064392 | tf_op jit(solution)/shard_map/ppermute | solution.py:78
  173.4 35.8 %collective-permute-start.52 = (bf16[384,896]{1,0:T(8,128)(2,1)S(1)}, bf16[384,896]{1,0:T(8,128)(2,1)S(1)}, u32[]{:S(2)}, u32[]{:S(2)}) collective-permute-start(bf16[384,896]{1,0:T(8,128)(2,1)S(1)} %fusion.21), channel_id=1, source_target_pairs={{0,2},{1,3},{2,0},{3,1},{4,6},{5,7},{6,4},{7,5},{8,10},{9,11},{10,... | collective-permute-start | bytes 2064392 | tf_op jit(solution)/shard_map/ppermute | solution.py:78
  200.3 69.3 %collective-permute-start.11 = (bf16[192,1024]{1,0:T(8,128)(2,1)}, bf16[192,1024]{1,0:T(8,128)(2,1)}, u32[]{:S(2)}, u32[]{:S(2)}) collective-permute-start(bf16[192,1024]{1,0:T(8,128)(2,1)} %select_convert_fusion.3), channel_id=1, source_target_pairs={{0,1},{1,0},{2,3},{3,2},{4,5},{5,4},{6,7},{7,6},{8,9},{9,8},{10,11... | collective-permute-start | bytes 1179656 | tf_op jit(solution)/shard_map/ppermute | solution.py:75
  214.4 35.9 %all-to-all-start.2 = ((bf16[4,160,2048]{2,1,0:T(8,128)(2,1)}), bf16[4,160,2048]{2,1,0:T(8,128)(2,1)}, u32[]{:S(2)}, u32[]{:S(2)}) async-start(bf16[4,160,2048]{2,1,0:T(8,128)(2,1)} %bitcast.105), calls=%async_computation.2 | async-start | bytes 5242880 | tf_op jit(solution)/shard_map/all_to_all | solution.py:107
  221.1 52.2 %collective-permute-start.53 = (bf16[192,1024]{1,0:T(8,128)(2,1)}, bf16[192,1024]{1,0:T(8,128)(2,1)}, u32[]{:S(2)}, u32[]{:S(2)}) collective-permute-start(bf16[192,1024]{1,0:T(8,128)(2,1)} %select_convert_fusion.2), channel_id=1, source_target_pairs={{0,1},{1,0},{2,3},{3,2},{4,5},{5,4},{6,7},{7,6},{8,9},{9,8},{10,11... | collective-permute-start | bytes 1179656 | tf_op jit(solution)/shard_map/ppermute | solution.py:75
  268.6 74.1 %collective-permute-start.23 = (bf16[2,640,896]{2,1,0:T(8,128)(2,1)S(1)}, bf16[2,640,896]{2,1,0:T(8,128)(2,1)S(1)}, u32[]{:S(2)}, u32[]{:S(2)}) collective-permute-start(bf16[2,640,896]{2,1,0:T(8,128)(2,1)S(1)} %slice.296), channel_id=1, source_target_pairs={{0,1},{1,0},{2,3},{3,2},{4,5},{5,4},{6,7},{7,6},{8,9},{9,8},{10,11... | collective-permute-start | bytes 6881288 | tf_op jit(solution)/shard_map/ppermute | solution.py:75
  268.8 32.6 %collective-permute-start.17 = (f32[320,256]{1,0:T(8,128)S(1)}, f32[320,256]{1,0:T(8,128)S(1)}, u32[]{:S(2)}, u32[]{:S(2)}) collective-permute-start(f32[320,256]{1,0:T(8,128)S(1)} %slice_select_fusion.1), channel_id=1, source_target_pairs={{0,1},{1,0},{2,3},{3,2},{4,5},{5,4},{6,7},{7,6},{8,9},{9,8},{10,11... | collective-permute-start | bytes 983048 | tf_op jit(solution)/shard_map/ppermute | solution.py:75
  287.5 58.7 %collective-permute-start.37 = (bf16[2,640,896]{2,1,0:T(8,128)(2,1)S(1)}, bf16[2,640,896]{2,1,0:T(8,128)(2,1)S(1)}, u32[]{:S(2)}, u32[]{:S(2)}) collective-permute-start(bf16[2,640,896]{2,1,0:T(8,128)(2,1)S(1)} %slice.309), channel_id=1, source_target_pairs={{0,1},{1,0},{2,3},{3,2},{4,5},{5,4},{6,7},{7,6},{8,9},{9,8},{10,11... | collective-permute-start | bytes 6881288 | tf_op jit(solution)/shard_map/ppermute | solution.py:75
  343.0 28.2 %collective-permute-start.24 = (bf16[640,896]{1,0:T(8,128)(2,1)S(1)}, bf16[640,896]{1,0:T(8,128)(2,1)S(1)}, u32[]{:S(2)}, u32[]{:S(2)}) collective-permute-start(bf16[640,896]{1,0:T(8,128)(2,1)S(1)} %fusion.16), channel_id=1, source_target_pairs={{0,2},{1,3},{2,0},{3,1},{4,6},{5,7},{6,4},{7,5},{8,10},{9,11},{10,... | collective-permute-start | bytes 3440648 | tf_op jit(solution)/shard_map/ppermute | solution.py:78
  346.6 48.2 %collective-permute-start.38 = (bf16[640,896]{1,0:T(8,128)(2,1)S(1)}, bf16[640,896]{1,0:T(8,128)(2,1)S(1)}, u32[]{:S(2)}, u32[]{:S(2)}) collective-permute-start(bf16[640,896]{1,0:T(8,128)(2,1)S(1)} %fusion.17), channel_id=1, source_target_pairs={{0,2},{1,3},{2,0},{3,1},{4,6},{5,7},{6,4},{7,5},{8,10},{9,11},{10,... | collective-permute-start | bytes 3440648 | tf_op jit(solution)/shard_map/ppermute | solution.py:78
  375.5 34.7 %collective-permute-start.25 = (bf16[320,1024]{1,0:T(8,128)(2,1)}, bf16[320,1024]{1,0:T(8,128)(2,1)S(1)}, u32[]{:S(2)}, u32[]{:S(2)}) collective-permute-start(bf16[320,1024]{1,0:T(8,128)(2,1)} %select_convert_fusion.1), channel_id=1, source_target_pairs={{0,1},{1,0},{2,3},{3,2},{4,5},{5,4},{6,7},{7,6},{8,9},{9,8},{10,11... | collective-permute-start | bytes 1966088 | tf_op jit(solution)/shard_map/ppermute | solution.py:75
  405.5 56.3 %all-to-all-start.4 = ((bf16[4,256,896]{2,1,0:T(8,128)(2,1)}), bf16[4,256,896]{2,1,0:T(8,128)(2,1)}, u32[]{:S(2)}, u32[]{:S(2)}) async-start(bf16[4,256,896]{2,1,0:T(8,128)(2,1)} %bitcast.103), calls=%async_computation.4 | async-start | bytes 3670016 | tf_op jit(solution)/shard_map/all_to_all | solution.py:224
  419.9 24.6 %collective-permute-start.41 = (bf16[320,256]{1,0:T(8,128)(2,1)S(1)}, bf16[320,256]{1,0:T(8,128)(2,1)S(1)}, u32[]{:S(2)}, u32[]{:S(2)}) collective-permute-start(bf16[320,256]{1,0:T(8,128)(2,1)S(1)} %get-tuple-element.28), channel_id=1, source_target_pairs={{0,8},{4,12},{8,0},{12,4},{1,9},{5,13},{9,1},{13,5},{2,10},{6,14},... | collective-permute-start | bytes 491528 | tf_op jit(solution)/shard_map/ppermute | solution.py:92
  (80 other events, 902.7 us)
Sparse Core Ops, SparseCore 0:
  10.1 39.7 all-gather.8
  52.1 35.8 all-gather.14
  89.5 53.5 all-gather.10
  144.6 61.2 all-gather.12
where the time goes:
time: 480 us; the launch traced here: 473 us
  waiting for transfers between devices  217 us (45%)
  starting transfers between devices  92.1 us (19%)
  Pallas kernels  55.6 us (12%)
  matrix products  40.8 us (8%)
  local copies, waits for them, and re-layouts  26.6 us (6%)
  other arithmetic  25 us (5%)
  between operations  15.3 us (3%)
    ppermute x12, waiting for transfers between devices, across(): lax.ppermute(array, 'token', [(i, (i // cores + step) % chips * cores + i...  100 us
    all_gather x4, waiting for transfers between devices, gathered_of(): return lax.all_gather(rows, 'neuron', axis=0)  67.1 us
    pallas_call x4, Pallas kernels, column_blocks(): pl.pallas_call(blocks_kernel, grid_spec=pltpu.PrefetchScalarGridSpec(num_...  55.6 us
    ppermute x24, starting transfers between devices, upward(): lax.ppermute(array, 'neuron', [(i, (i + step) % neurons_on) for i in rang...  46.5 us
    ppermute x24, waiting for transfers between devices, upward(): lax.ppermute(array, 'neuron', [(i, (i + step) % neurons_on) for i in rang...  42.6 us
    dot_general x20, matrix products, dot(): lax.dot_general(left, right, (dims, ((), ())), preferred_element_type=F32)  40.8 us
    ppermute x12, starting transfers between devices, across(): lax.ppermute(array, 'token', [(i, (i // cores + step) % chips * cores + i...  18.9 us
    all_to_all x4, starting transfers between devices, spread_of(): lax.all_to_all(gathered, 'token', split_axis=0, concat_axis=0, tiled=True)  16.2 us
  transfers between devices with their start and end apart: 68, of which 28 were waited for; matrix products, arithmetic and copies ran while one was open for 16% of the time, Pallas kernels for 12%

commit v1 on v0

v1 whole, which is shorter than its diff:
```python
import math

import jax
import jax.numpy as jnp
from jax import lax
from jax.experimental import pallas as pl
from jax.experimental.pallas import tpu as pltpu
from jax.sharding import PartitionSpec as P


SHARES = (6, 10, 10, 6)
CHUNKS = len(SHARES)
F32 = jnp.float32
BF16 = jnp.bfloat16


def dot(left, right, dims=((1,), (0,))):
    return lax.dot_general(left, right, (dims, ((), ())), preferred_element_type=F32)


def block(array, start, size, axis):
    starts = [start if d == axis else 0 for d in range(array.ndim)]
    sizes = [size if d == axis else n for d, n in enumerate(array.shape)]
    return lax.dynamic_slice(array, starts, sizes, allow_negative_indices=False)


def blocks_kernel(order_ref, left_ref, right_ref, sent_ref, kept_ref):
    rows = left_ref.shape[0]
    step = rows // 2 if rows % 32 == 0 else rows

    def fill(out_ref):
        for start in range(0, rows, step):
            at = pl.ds(start, step)
            out_ref[0, at, :] = jnp.dot(
                left_ref[at, :], right_ref[...], preferred_element_type=F32
            ).astype(BF16)

    first = pl.program_id(0) < pl.num_programs(0) // 2
    pl.when(first)(lambda: fill(sent_ref))
    pl.when(jnp.logical_not(first))(lambda: fill(kept_ref))


def column_blocks(left, right, order, columns):
    rows, depth = left.shape
    count = order.shape[0]
    half = count // 2
    shape = jax.ShapeDtypeStruct((half, rows, columns), BF16)
    return pl.pallas_call(
        blocks_kernel,
        grid_spec=pltpu.PrefetchScalarGridSpec(
            num_scalar_prefetch=1,
            grid=(count,),
            in_specs=[
                pl.BlockSpec((rows, depth), lambda j, order: (0, 0)),
                pl.BlockSpec((depth, columns), lambda j, order: (0, order[j])),
            ],
            out_specs=[
                pl.BlockSpec((1, rows, columns), lambda j, order: (jnp.minimum(j, half - 1), 0, 0)),
                pl.BlockSpec((1, rows, columns), lambda j, order: (jnp.maximum(j - half, 0), 0, 0)),
            ],
        ),
        out_shape=[shape, shape],
        compiler_params=pltpu.CompilerParams(vmem_limit_bytes=32 << 20),
        cost_estimate=pl.CostEstimate(
            flops=2 * rows * depth * columns * count,
            bytes_accessed=2 * (rows * depth + (depth + rows) * columns * count),
            transcendentals=0,
        ),
    )(order, left, pltpu.with_memory_space_constraint(right, pltpu.HBM))


def arrange_kernel(order_ref, *refs):
    *in_refs, out_ref = refs
    core = order_ref[pl.num_programs(0)]
    for at, (first, second) in ((core, in_refs[::2]), (1 - core, in_refs[1::2])):
        out_ref[0, pl.ds(at, 1)] = (first[...] + second[...]).astype(BF16)


def arranged(early, late, order, count):
    rows, columns = early[0].shape[0] // count, early[0].shape[1]
    spec = pl.BlockSpec((1, rows, columns), lambda p, order: (order[p], 0, 0))
    return pl.pallas_call(
        arrange_kernel,
        grid_spec=pltpu.PrefetchScalarGridSpec(
            num_scalar_prefetch=1,
            grid=(count,),
            in_specs=[spec] * 4,
            out_specs=pl.BlockSpec((1, 2, rows, columns), lambda p, order: (p, 0, 0, 0)),
        ),
        out_shape=jax.ShapeDtypeStruct((count, 2, rows, columns), BF16),
        cost_estimate=pl.CostEstimate(
            flops=0, bytes_accessed=20 * count * rows * columns, transcendentals=0
        ),
    )(order, *(one.reshape(count, rows, columns) for one in (*early, *late)))


def per_device(tokens, up_weight, encoder, decoder):
    row_count, width = tokens.shape
    tokens_on, neurons_on = lax.axis_size("token"), lax.axis_size("neuron")
    cores, chips = 2, tokens_on // 2
    total_rows = row_count * tokens_on
    me = lax.axis_index("token")
    plane = lax.axis_index("neuron")
    chip, core = lax.div(me, cores), lax.rem(me, cores)
    columns = up_weight.shape[1] // tokens_on
    ranks = encoder.shape[1]
    split = ranks // cores
    edges = [row_count * sum(SHARES[:k]) // sum(SHARES) for k in range(len(SHARES) + 1)]
    planes = [lax.rem(plane + neurons_on - j, neurons_on) for j in range(neurons_on)]

    def exchange(array, step, other):
        pairs = [
            (i, (i // cores + step) % chips * cores + (i % cores ^ other))
            for i in range(tokens_on)
        ]
        return lax.ppermute(array, "token", pairs)

    def swap(array):
        return exchange(array, 0, 1)

    def across(array, step):
        return exchange(array, step, 0)

    def upward(array, step):
        return lax.ppermute(
            array, "neuron", [(i, (i + step) % neurons_on) for i in range(neurons_on)]
        )

    def cut(array, j):
        return lax.slice_in_dim(array, j * split, (j + 1) * split, axis=1)

    def gathered_of(k):
        rows = tokens[edges[k] : edges[k + 1]]
        if neurons_on % tokens_on == 0:
            return lax.all_gather(rows, "neuron", axis=0)
        return lax.all_gather(rows, "neuron", axis=1, tiled=True)

    def spread_of(gathered):
        if neurons_on % tokens_on:
            return lax.all_to_all(
                gathered, "token", split_axis=1, concat_axis=0, tiled=True
            )
        moved = lax.all_to_all(gathered, "token", split_axis=0, concat_axis=0, tiled=True)
        ratio = neurons_on // tokens_on
        if ratio == 1:
            return moved.reshape(-1, width)
        moved = moved.reshape(tokens_on, ratio, -1, width)
        return moved.transpose(0, 2, 1, 3).reshape(-1, ratio * width)

    def partials_of(piece):
        steps = list(range(1, chips)) + [0]
        order = [
            lax.rem(chip + step, chips) * cores + (core ^ other)
            for other in (1, 0)
            for step in steps
        ]
        if columns % 128 == 0:
            return column_blocks(piece, up_weight, jnp.stack(order), columns)
        terms = [
            dot(piece, block(up_weight, at * columns, columns, 1)).astype(BF16) for at in order
        ]
        return jnp.stack(terms[:chips]), jnp.stack(terms[chips:])

    def labels_of(piece):
        sent, kept = partials_of(piece)
        moved = swap(sent)
        kept = [kept[j].astype(F32) + moved[j].astype(F32) for j in range(chips)]
        total = kept[chips - 1]
        for step in range(1, chips):
            moved = across(kept[step - 1].astype(BF16), step)
            total = total + moved.astype(F32)
        return total

    def hidden_of(piece, encoder_own):
        terms = dot(piece, encoder_own)
        moved = swap(cut(terms, 0))
        summed = cut(terms, 1) + moved
        whole = summed
        for step in range(1, chips):
            moved = across(summed.astype(BF16), step)
            whole = whole + moved.astype(F32)
        shared = [whole.astype(BF16)]
        for step in range(1, neurons_on):
            shared.append(upward(shared[0], step))
        mine = jnp.concatenate(shared, axis=1)
        return mine, swap(mine)

    def back_of(scaled, decoders):
        terms = dot(scaled, decoders[1], ((1,), (1,))).astype(BF16)
        moved = swap(terms)
        terms = dot(scaled, decoders[0], ((1,), (1,)))
        terms = terms + moved.astype(F32)
        own = cut(terms, 0)
        for step in range(1, neurons_on):
            sent = cut(terms, neurons_on - step).astype(BF16)
            moved = upward(sent, step)
            own = own + moved.astype(F32)
        whole = own
        for step in range(1, chips):
            moved = across(own.astype(BF16), step)
            whole = whole + moved.astype(F32)
        mine = whole.astype(BF16)
        theirs = swap(mine)
        return jnp.concatenate([mine, theirs], axis=1)

    gathered = [gathered_of(k) for k in range(CHUNKS)]
    arrived = []
    for step in range(chips):
        for other in range(cores):
            there = lax.rem(chip + step, chips) * cores + (core ^ other)
            sent = block(decoder, there * columns, columns, 1)
            if step or other:
                sent = exchange(sent, step, other)
            arrived.append(sent)
    rows = []
    for j in range(tokens_on):
        which = lax.rem(chip + chips - j // cores, chips) * cores + (core ^ (j % cores))
        rows.append(lax.select_n(which, *arrived))
    rows = jnp.concatenate(rows, axis=0)
    decoders = [
        jnp.concatenate([block(rows, at * ranks + part * split, split, 0) for at in planes], axis=0)
        for part in (core, 1 - core)
    ]
    encoder_own = jnp.concatenate(
        [block(encoder, part * split, split, 1) for part in (1 - core, core)], axis=1
    )
    grad_encoder = None
    for k in range(CHUNKS):
        piece = spread_of(gathered[k])
        labels = jax.nn.relu(labels_of(piece))
        hiddens = hidden_of(piece, encoder_own)
        predicted = dot(hiddens[0], decoders[0]) + dot(hiddens[1], decoders[1])
        scaled = ((predicted - labels) / math.sqrt(total_rows)).astype(BF16)
        terms = [dot(hidden, scaled, ((0,), (0,))) for hidden in hiddens]
        if k == CHUNKS - 1:
            late_terms = terms
        elif k:
            earlier = lax.optimization_barrier(early_terms)
            early_terms = [one + two for one, two in zip(earlier, terms)]
        else:
            early_terms = terms
        back = back_of(scaled, decoders)
        term = dot(piece, back, ((0,), (0,)))
        if grad_encoder is not None:
            term = lax.optimization_barrier(grad_encoder) + term
        grad_encoder = term
    grad_decoder = arranged(early_terms, late_terms, jnp.stack(planes + [core]), neurons_on)
    grad_decoder = lax.all_to_all(
        grad_decoder.reshape(tokens_on, -1, columns),
        "token",
        split_axis=0,
        concat_axis=0,
        tiled=True,
    )
    grad_decoder = jnp.concatenate([grad_decoder[j] for j in range(tokens_on)], axis=1)
    parts = [grad_encoder[:, :split], grad_encoder[:, split:]]
    grad_encoder = jnp.concatenate(
        [jnp.where(core == 0, *parts), jnp.where(core == 0, *parts[::-1])], axis=1
    )
    return (grad_encoder, grad_decoder.astype(F32))


def solution(mesh):
    return jax.shard_map(
        per_device,
        mesh=mesh,
        in_specs=(P(("layer", "token"), "neuron"),) * 4,
        out_specs=(P(("layer", "token"), "neuron"),) * 2,
        check_vma=False,
    )
```

time: 480 us -> 482 us (level)
  waiting for transfers between devices: 217 us -> 250 us
  starting transfers between devices: 92.1 us -> 69.7 us
  other arithmetic: 25 us -> 13.6 us
  local copies, waits for them, and re-layouts: 26.6 us -> 18.3 us
  matrix products: 40.8 us -> 47.3 us
    ppermute x32 -> x0, waiting for transfers between devices: 103 us -> none  [the longest x12 100 us: across(): lax.ppermute(array, 'token', [(i, (i // cores + step) % chips * cores + i...]
    ppermute x3 -> x35, waiting for transfers between devices: 0.01 us -> 98.2 us  [exchange(): return lax.ppermute(array, 'token', pairs)]
    ppermute x32 -> x0, starting transfers between devices: 22.5 us -> none  [the longest x12 18.9 us: across(): lax.ppermute(array, 'token', [(i, (i // cores + step) % chips * cores + i...]
    all_gather x4, waiting for transfers between devices: 67.1 us -> 84.7 us  [gathered_of(): return lax.all_gather(rows, 'neuron', axis=0)]
    ppermute x24, waiting for transfers between devices: 42.6 us -> 58.2 us  [upward(): lax.ppermute(array, 'neuron', [(i, (i + step) % neurons_on) for i in rang...]
    ppermute x3 -> x35, starting transfers between devices: 2.14 us -> 17 us  [exchange(): return lax.ppermute(array, 'token', pairs)]
    ppermute x24, starting transfers between devices: 46.5 us -> 33.6 us  [upward(): lax.ppermute(array, 'neuron', [(i, (i + step) % neurons_on) for i in rang...]
    unnamed x73 -> x117, local copies, waits for them, and re-layouts: 15.2 us -> 6.91 us
  transfers between devices with their start and end apart: 68 -> 68, of which waited for: 28 -> 27; matrix products, arithmetic and copies ran while one was open for 16% -> 14% of each run, Pallas kernels for 12% -> 12%
where the time goes in v1:
time: 482 us; the launch traced here: 472 us
  waiting for transfers between devices  250 us (52%)
  starting transfers between devices  69.7 us (14%)
  Pallas kernels  58 us (12%)
  matrix products  47.3 us (10%)
  local copies, waits for them, and re-layouts  18.3 us (4%)
  between operations  15.4 us (3%)
  other arithmetic  13.6 us (3%)
    ppermute x35, waiting for transfers between devices, exchange(): return lax.ppermute(array, 'token', pairs)  98.2 us
    all_gather x4, waiting for transfers between devices, gathered_of(): return lax.all_gather(rows, 'neuron', axis=0)  84.7 us
    ppermute x24, waiting for transfers between devices, upward(): lax.ppermute(array, 'neuron', [(i, (i + step) % neurons_on) for i in rang...  58.2 us
    pallas_call x4, Pallas kernels, column_blocks(): pl.pallas_call(blocks_kernel, grid_spec=pltpu.PrefetchScalarGridSpec(num_...  52.4 us
    dot_general x32, matrix products, dot(): lax.dot_general(left, right, (dims, ((), ())), preferred_element_type=F32)  47.3 us
    ppermute x24, starting transfers between devices, upward(): lax.ppermute(array, 'neuron', [(i, (i + step) % neurons_on) for i in rang...  33.6 us
    ppermute x35, starting transfers between devices, exchange(): return lax.ppermute(array, 'token', pairs)  17 us
    all_to_all x4, starting transfers between devices, spread_of(): lax.all_to_all(gathered, 'token', split_axis=0, concat_axis=0, tiled=True)  14.4 us
  transfers between devices with their start and end apart: 68, of which 27 were waited for; matrix products, arithmetic and copies ran while one was open for 14% of the time, Pallas kernels for 12%

profile of v1, /device:TPU:0, one launch (start us, length us, event | category | flops | bytes accessed | tf_op | source)
XLA Modules:
  0.0 472.3 jit_solution(6028515630386603416)
XLA Ops:
  11.4 38.5 %all-gather.9.cloned.1.call-done = bf16[384,2048]{1,0:T(8,128)(2,1)} async-done(((bf16[96,2048]{1,0:T(8,128)(2,1)}), bf16[384,2048]{1,0:T(8,128)(2,1)}) %all-gather.9.cloned.1.call-update) | async-done | bytes 1572880 | tf_op jit(solution)/shard_map/all_gather | solution.py:135
  60.1 27.8 %all-gather.15.cloned.1.call-done = bf16[384,2048]{1,0:T(8,128)(2,1)} async-done(((bf16[96,2048]{1,0:T(8,128)(2,1)}), bf16[384,2048]{1,0:T(8,128)(2,1)}) %all-gather.15.cloned.1.call-update) | async-done | bytes 1572880 | tf_op jit(solution)/shard_map/all_gather | solution.py:135
  96.1 11.4 %shard_map.59 = (bf16[2,384,896]{2,1,0:T(8,128)(2,1)}, bf16[2,384,896]{2,1,0:T(8,128)(2,1)S(1)}) custom-call(s32[4]{0:T(128)S(1)} %pad_add_fusion.order_ref, bf16[384,2048]{1,0:T(8,128)(2,1)S(1)} %bitcast.135, bf16[2048,3584]{1,0:T(8,128)(2,1)} %right_ref.7), custom_call_target="tpu_custom_call" | custom-call | flops 5637144576 | bytes 19005440 | tf_op jit(solution)/shard_map/pallas_call | solution.py:48
  111.6 11.7 %shard_map.62 = (bf16[2,384,896]{2,1,0:T(8,128)(2,1)}, bf16[2,384,896]{2,1,0:T(8,128)(2,1)S(1)}) custom-call(s32[4]{0:T(128)S(1)} %pad_add_fusion.order_ref, bf16[384,2048]{1,0:T(8,128)(2,1)S(1)} %bitcast.132, bf16[2048,3584]{1,0:T(8,128)(2,1)} %right_ref.7), custom_call_target="tpu_custom_call" | custom-call | flops 5637144576 | bytes 19005440 | tf_op jit(solution)/shard_map/pallas_call | solution.py:48
  133.1 18.4 %all-gather.11.cloned.1.call-done = bf16[640,2048]{1,0:T(8,128)(2,1)} async-done(((bf16[160,2048]{1,0:T(8,128)(2,1)}), bf16[640,2048]{1,0:T(8,128)(2,1)}) %all-gather.11.cloned.1.call-update) | async-done | bytes 2621456 | tf_op jit(solution)/shard_map/all_gather | solution.py:135
  161.1 12.5 %collective-permute-done.48 = bf16[384,128]{0,1:T(8,128)(2,1)S(1)} collective-permute-done((bf16[384,128]{0,1:T(8,128)(2,1)S(1)}, bf16[384,128]{0,1:T(8,128)(2,1)S(1)}, u32[]{:S(2)}, u32[]{:S(2)}) %collective-permute-start.48) | collective-permute-done | bytes 98336 | tf_op jit(solution)/shard_map/ppermute | solution.py:125
  179.8 22.0 %collective-permute-done.10 = bf16[384,896]{1,0:T(8,128)(2,1)S(1)} collective-permute-done((bf16[384,896]{1,0:T(8,128)(2,1)S(1)}, bf16[384,896]{1,0:T(8,128)(2,1)S(1)}, u32[]{:S(2)}, u32[]{:S(2)}) %collective-permute-start.10) | collective-permute-done | bytes 688160 | tf_op jit(solution)/shard_map/ppermute | solution.py:116
  205.1 10.8 %collective-permute-done.52 = bf16[384,896]{1,0:T(8,128)(2,1)S(1)} collective-permute-done((bf16[384,896]{1,0:T(8,128)(2,1)S(1)}, bf16[384,896]{1,0:T(8,128)(2,1)S(1)}, u32[]{:S(2)}, u32[]{:S(2)}) %collective-permute-start.52) | collective-permute-done | bytes 688160 | tf_op jit(solution)/shard_map/ppermute | solution.py:116
  233.4 15.3 %shard_map.60 = (bf16[2,640,896]{2,1,0:T(8,128)(2,1)}, bf16[2,640,896]{2,1,0:T(8,128)(2,1)S(1)}) custom-call(s32[4]{0:T(128)S(1)} %pad_add_fusion.order_ref, bf16[640,2048]{1,0:T(8,128)(2,1)S(1)} %bitcast.129, bf16[2048,3584]{1,0:T(8,128)(2,1)} %right_ref.7), custom_call_target="tpu_custom_call" | custom-call | flops 9395240960 | bytes 21889024 | tf_op jit(solution)/shard_map/pallas_call | solution.py:48
  251.3 6.2 %all-to-all-done.2 = bf16[4,160,2048]{2,1,0:T(8,128)(2,1)S(1)} async-done(((bf16[4,160,2048]{2,1,0:T(8,128)(2,1)}), bf16[4,160,2048]{2,1,0:T(8,128)(2,1)S(1)}, u32[]{:S(2)}, u32[]{:S(2)}) %all-to-all-start.2) | async-done | bytes 2621472 | tf_op jit(solution)/shard_map/all_to_all | solution.py:143
  257.6 14.2 %shard_map.61 = (bf16[2,640,896]{2,1,0:T(8,128)(2,1)S(1)}, bf16[2,640,896]{2,1,0:T(8,128)(2,1)S(1)}) custom-call(s32[4]{0:T(128)S(1)} %pad_add_fusion.order_ref, bf16[640,2048]{1,0:T(8,128)(2,1)S(1)} %bitcast.126, bf16[2048,3584]{1,0:T(8,128)(2,1)} %right_ref.7), custom_call_target="tpu_custom_call" | custom-call | flops 9395240960 | bytes 21889024 | tf_op jit(solution)/shard_map/pallas_call | solution.py:48
  287.8 5.4 %collective-permute-done.55 = bf16[384,128]{1,0:T(8,128)(2,1)S(1)} collective-permute-done((bf16[384,128]{1,0:T(8,128)(2,1)S(1)}, bf16[384,128]{1,0:T(8,128)(2,1)S(1)}, u32[]{:S(2)}, u32[]{:S(2)}) %collective-permute-start.55) | collective-permute-done | bytes 98336 | tf_op jit(solution)/shard_map/ppermute | solution.py:125
  294.1 4.3 collective-permute-done.15
  305.4 4.9 %collective-permute-done.18 = bf16[640,128]{0,1:T(8,128)(2,1)S(1)} collective-permute-done((bf16[640,128]{0,1:T(8,128)(2,1)S(1)}, bf16[640,128]{0,1:T(8,128)(2,1)S(1)}, u32[]{:S(2)}, u32[]{:S(2)}) %collective-permute-start.18) | collective-permute-done | bytes 163872 | tf_op jit(solution)/shard_map/ppermute | solution.py:116
  320.5 6.9 %collective-permute-done.20 = bf16[640,128]{0,1:T(8,128)(2,1)S(1)} collective-permute-done((bf16[640,128]{0,1:T(8,128)(2,1)S(1)}, bf16[640,128]{0,1:T(8,128)(2,1)S(1)}, u32[]{:S(2)}, u32[]{:S(2)}) %collective-permute-start.20) | collective-permute-done | bytes 163872 | tf_op jit(solution)/shard_map/ppermute | solution.py:125
  327.5 6.0 %collective-permute-start.33 = (bf16[640,128]{0,1:T(8,128)(2,1)S(1)}, bf16[640,128]{0,1:T(8,128)(2,1)S(1)}, u32[]{:S(2)}, u32[]{:S(2)}) collective-permute-start(bf16[640,128]{0,1:T(8,128)(2,1)S(1)} %add_convert_fusion.5), channel_id=1, source_target_pairs={{0,4},{4,8},{8,12},{12,0},{1,5},{5,9},{9,13},{13,1},{2,6},{6,10},{... | collective-permute-start | bytes 491528 | tf_op jit(solution)/shard_map/ppermute | solution.py:125
  335.7 4.3 collective-permute-done.34
  348.3 22.2 %collective-permute-done.24 = bf16[640,896]{1,0:T(8,128)(2,1)S(1)} collective-permute-done((bf16[640,896]{1,0:T(8,128)(2,1)S(1)}, bf16[640,896]{1,0:T(8,128)(2,1)S(1)}, u32[]{:S(2)}, u32[]{:S(2)}) %collective-permute-start.24) | collective-permute-done | bytes 1146912 | tf_op jit(solution)/shard_map/ppermute | solution.py:116
  374.4 19.7 %collective-permute-done.38 = bf16[640,896]{1,0:T(8,128)(2,1)S(1)} collective-permute-done((bf16[640,896]{1,0:T(8,128)(2,1)S(1)}, bf16[640,896]{1,0:T(8,128)(2,1)S(1)}, u32[]{:S(2)}, u32[]{:S(2)}) %collective-permute-start.38) | collective-permute-done | bytes 1146912 | tf_op jit(solution)/shard_map/ppermute | solution.py:116
  403.7 5.5 %shard_map.63 = bf16[4,2,128,896]{3,2,1,0:T(8,128)(2,1)} custom-call(s32[5]{0:T(128)} %stack.58.order_ref, f32[4,128,896]{2,1,0:T(8,128)} %bitcast.142, f32[4,128,896]{2,1,0:T(8,128)} %bitcast.141, f32[4,128,896]{2,1,0:T(8,128)} %bitcast.139, f32[4,128,896]{2,1,0:T(8,128)} %bitcast.140), custom_call_target="tpu_custom_call" | custom-call | bytes 9175040 | tf_op jit(solution)/shard_map/pallas_call | solution.py:82
  409.2 4.5 all-to-all-start.4
  427.1 7.6 %collective-permute-done.27 = bf16[640,128]{0,1:T(8,128)(2,1)S(1)} collective-permute-done((bf16[640,128]{0,1:T(8,128)(2,1)S(1)}, bf16[640,128]{0,1:T(8,128)(2,1)S(1)}, u32[]{:S(2)}, u32[]{:S(2)}) %collective-permute-start.27) | collective-permute-done | bytes 163872 | tf_op jit(solution)/shard_map/ppermute | solution.py:125
  436.8 11.4 %collective-permute-done.41 = bf16[640,128]{0,1:T(8,128)(2,1)S(1)} collective-permute-done((bf16[640,128]{0,1:T(8,128)(2,1)S(1)}, bf16[640,128]{0,1:T(8,128)(2,1)S(1)}, u32[]{:S(2)}, u32[]{:S(2)}) %collective-permute-start.41) | collective-permute-done | bytes 163872 | tf_op jit(solution)/shard_map/ppermute | solution.py:125
  450.3 3.9 collective-permute-done.43
  (318 shorter events, 161.4 us)
Async XLA Ops:
  7.2 42.7 %all-gather.9.cloned.1.call-start = ((), (), s32[]{:S(2)}) async-start(), calls=%async_computation.5 | async-start | bytes 1966080 | tf_op jit(solution)/shard_map/all_gather | solution.py:135
  9.4 78.5 %all-gather.15.cloned.1.call-start = ((), (), s32[]{:S(2)}) async-start(), calls=%async_computation.8 | async-start | bytes 1966080 | tf_op jit(solution)/shard_map/all_gather | solution.py:135
  10.2 141.3 %all-gather.11.cloned.1.call-start = ((), (), s32[]{:S(2)}) async-start(), calls=%async_computation.6 | async-start | bytes 3276800 | tf_op jit(solution)/shard_map/all_gather | solution.py:135
  49.9 38.1 %all-to-all-start = ((bf16[4,96,2048]{2,1,0:T(8,128)(2,1)}), bf16[4,96,2048]{2,1,0:T(8,128)(2,1)S(1)}, u32[]{:S(2)}, u32[]{:S(2)}) async-start(bf16[4,96,2048]{2,1,0:T(8,128)(2,1)} %bitcast.146), calls=%async_computation | async-start | bytes 3145728 | tf_op jit(solution)/shard_map/all_to_all | solution.py:143
  53.5 167.7 %all-gather.13.cloned.1.call-start = ((), (), s32[]{:S(2)}) async-start(), calls=%async_computation.7 | async-start | bytes 3276800 | tf_op jit(solution)/shard_map/all_gather | solution.py:135
  56.1 35.5 %collective-permute-start.6 = (bf16[256,896]{1,0:T(8,128)(2,1)}, bf16[256,896]{1,0:T(8,128)(2,1)}, u32[]{:S(2)}, u32[]{:S(2)}) collective-permute-start(bf16[256,896]{1,0:T(8,128)(2,1)} %get-tuple-element.52), channel_id=1, source_target_pairs={{0,2},{1,3},{2,0},{3,1},{4,6},{5,7},{6,4},{7,5},{8,10},{9,11},{10,... | collective-permute-start | bytes 1376264 | tf_op jit(solution)/shard_map/ppermute | solution.py:116
  58.0 34.7 %collective-permute-start.7 = (bf16[256,896]{1,0:T(8,128)(2,1)}, bf16[256,896]{1,0:T(8,128)(2,1)}, u32[]{:S(2)}, u32[]{:S(2)}) collective-permute-start(bf16[256,896]{1,0:T(8,128)(2,1)} %get-tuple-element.51), channel_id=1, source_target_pairs={{0,3},{1,2},{2,1},{3,0},{4,7},{5,6},{6,5},{7,4},{8,11},{9,10},{10,... | collective-permute-start | bytes 1376264 | tf_op jit(solution)/shard_map/ppermute | solution.py:116
  58.0 34.7 %collective-permute-start.5 = (bf16[256,896]{1,0:T(8,128)(2,1)}, bf16[256,896]{1,0:T(8,128)(2,1)}, u32[]{:S(2)}, u32[]{:S(2)}) collective-permute-start(bf16[256,896]{1,0:T(8,128)(2,1)} %get-tuple-element.50), channel_id=1, source_target_pairs={{0,1},{1,0},{2,3},{3,2},{4,5},{5,4},{6,7},{7,6},{8,9},{9,8},{10,11... | collective-permute-start | bytes 1376264 | tf_op jit(solution)/shard_map/ppermute | solution.py:116
  107.5 66.2 %collective-permute-start.9 = (bf16[2,384,896]{2,1,0:T(8,128)(2,1)}, bf16[2,384,896]{2,1,0:T(8,128)(2,1)}, u32[]{:S(2)}, u32[]{:S(2)}) collective-permute-start(bf16[2,384,896]{2,1,0:T(8,128)(2,1)} %get-tuple-element.15), channel_id=1, source_target_pairs={{0,1},{1,0},{2,3},{3,2},{4,5},{5,4},{6,7},{7,6},{8,9},{9,8},{10,11... | collective-permute-start | bytes 4128776 | tf_op jit(solution)/shard_map/ppermute | solution.py:116
  123.2 52.5 %collective-permute-start.51 = (bf16[2,384,896]{2,1,0:T(8,128)(2,1)}, bf16[2,384,896]{2,1,0:T(8,128)(2,1)}, u32[]{:S(2)}, u32[]{:S(2)}) collective-permute-start(bf16[2,384,896]{2,1,0:T(8,128)(2,1)} %get-tuple-element.21), channel_id=1, source_target_pairs={{0,1},{1,0},{2,3},{3,2},{4,5},{5,4},{6,7},{7,6},{8,9},{9,8},{10,11... | collective-permute-start | bytes 4128776 | tf_op jit(solution)/shard_map/ppermute | solution.py:116
  151.5 69.6 %all-to-all-start.1 = ((bf16[4,160,2048]{2,1,0:T(8,128)(2,1)}), bf16[4,160,2048]{2,1,0:T(8,128)(2,1)S(1)}, u32[]{:S(2)}, u32[]{:S(2)}) async-start(bf16[4,160,2048]{2,1,0:T(8,128)(2,1)} %bitcast.143), calls=%async_computation.1 | async-start | bytes 5242880 | tf_op jit(solution)/shard_map/all_to_all | solution.py:143
  175.0 26.7 %collective-permute-start.10 = (bf16[384,896]{1,0:T(8,128)(2,1)S(1)}, bf16[384,896]{1,0:T(8,128)(2,1)S(1)}, u32[]{:S(2)}, u32[]{:S(2)}) collective-permute-start(bf16[384,896]{1,0:T(8,128)(2,1)S(1)} %fusion.20), channel_id=1, source_target_pairs={{0,2},{1,3},{2,0},{3,1},{4,6},{5,7},{6,4},{7,5},{8,10},{9,11},{10,... | collective-permute-start | bytes 2064392 | tf_op jit(solution)/shard_map/ppermute | solution.py:116
  177.7 38.3 %collective-permute-start.52 = (bf16[384,896]{1,0:T(8,128)(2,1)S(1)}, bf16[384,896]{1,0:T(8,128)(2,1)S(1)}, u32[]{:S(2)}, u32[]{:S(2)}) collective-permute-start(bf16[384,896]{1,0:T(8,128)(2,1)S(1)} %fusion.21), channel_id=1, source_target_pairs={{0,2},{1,3},{2,0},{3,1},{4,6},{5,7},{6,4},{7,5},{8,10},{9,11},{10,... | collective-permute-start | bytes 2064392 | tf_op jit(solution)/shard_map/ppermute | solution.py:116
  205.1 67.8 %collective-permute-start.11 = (bf16[384,512]{1,0:T(8,128)(2,1)}, bf16[384,512]{1,0:T(8,128)(2,1)}, u32[]{:S(2)}, u32[]{:S(2)}) collective-permute-start(bf16[384,512]{1,0:T(8,128)(2,1)} %convolution_convert_fusion.3), channel_id=1, source_target_pairs={{0,1},{1,0},{2,3},{3,2},{4,5},{5,4},{6,7},{7,6},{8,9},{9,8},{10,11... | collective-permute-start | bytes 1179656 | tf_op jit(solution)/shard_map/ppermute | solution.py:116
  219.2 56.5 %collective-permute-start.53 = (bf16[384,512]{1,0:T(8,128)(2,1)}, bf16[384,512]{1,0:T(8,128)(2,1)}, u32[]{:S(2)}, u32[]{:S(2)}) collective-permute-start(bf16[384,512]{1,0:T(8,128)(2,1)} %convolution_convert_fusion.2), channel_id=1, source_target_pairs={{0,1},{1,0},{2,3},{3,2},{4,5},{5,4},{6,7},{7,6},{8,9},{9,8},{10,11... | collective-permute-start | bytes 1179656 | tf_op jit(solution)/shard_map/ppermute | solution.py:116
  222.6 34.9 %all-to-all-start.2 = ((bf16[4,160,2048]{2,1,0:T(8,128)(2,1)}), bf16[4,160,2048]{2,1,0:T(8,128)(2,1)S(1)}, u32[]{:S(2)}, u32[]{:S(2)}) async-start(bf16[4,160,2048]{2,1,0:T(8,128)(2,1)} %bitcast.144), calls=%async_computation.2 | async-start | bytes 5242880 | tf_op jit(solution)/shard_map/all_to_all | solution.py:143
  248.6 92.1 %collective-permute-start.23 = (bf16[2,640,896]{2,1,0:T(8,128)(2,1)}, bf16[2,640,896]{2,1,0:T(8,128)(2,1)}, u32[]{:S(2)}, u32[]{:S(2)}) collective-permute-start(bf16[2,640,896]{2,1,0:T(8,128)(2,1)} %get-tuple-element.17), channel_id=1, source_target_pairs={{0,1},{1,0},{2,3},{3,2},{4,5},{5,4},{6,7},{7,6},{8,9},{9,8},{10,11... | collective-permute-start | bytes 6881288 | tf_op jit(solution)/shard_map/ppermute | solution.py:116
  251.1 52.1 %collective-permute-start.17 = (f32[640,128]{0,1:T(8,128)S(1)}, f32[640,128]{0,1:T(8,128)S(1)}, u32[]{:S(2)}, u32[]{:S(2)}) collective-permute-start(f32[640,128]{0,1:T(8,128)S(1)} %slice.221), channel_id=1, source_target_pairs={{0,1},{1,0},{2,3},{3,2},{4,5},{5,4},{6,7},{7,6},{8,9},{9,8},{10,11... | collective-permute-start | bytes 983048 | tf_op jit(solution)/shard_map/ppermute | solution.py:116
  287.8 57.1 %collective-permute-start.37 = (bf16[2,640,896]{2,1,0:T(8,128)(2,1)S(1)}, bf16[2,640,896]{2,1,0:T(8,128)(2,1)S(1)}, u32[]{:S(2)}, u32[]{:S(2)}) collective-permute-start(bf16[2,640,896]{2,1,0:T(8,128)(2,1)S(1)} %get-tuple-element.19), channel_id=1, source_target_pairs={{0,1},{1,0},{2,3},{3,2},{4,5},{5,4},{6,7},{7,6},{8,9},{9,8},{10,11... | collective-permute-start | bytes 6881288 | tf_op jit(solution)/shard_map/ppermute | solution.py:116
  335.6 121.6 %collective-permute-start.58 = (bf16[384,128]{1,0:T(8,128)(2,1)S(1)}, bf16[384,128]{1,0:T(8,128)(2,1)}, u32[]{:S(2)}, u32[]{:S(2)}) collective-permute-start(bf16[384,128]{1,0:T(8,128)(2,1)S(1)} %add_convert_fusion.8), channel_id=1, source_target_pairs={{0,1},{1,0},{2,3},{3,2},{4,5},{5,4},{6,7},{7,6},{8,9},{9,8},{10,11... | collective-permute-start | bytes 294920 | tf_op jit(solution)/shard_map/ppermute | solution.py:116
  342.2 28.2 %collective-permute-start.24 = (bf16[640,896]{1,0:T(8,128)(2,1)S(1)}, bf16[640,896]{1,0:T(8,128)(2,1)S(1)}, u32[]{:S(2)}, u32[]{:S(2)}) collective-permute-start(bf16[640,896]{1,0:T(8,128)(2,1)S(1)} %fusion.18), channel_id=1, source_target_pairs={{0,2},{1,3},{2,0},{3,1},{4,6},{5,7},{6,4},{7,5},{8,10},{9,11},{10,... | collective-permute-start | bytes 3440648 | tf_op jit(solution)/shard_map/ppermute | solution.py:116
  345.2 48.9 %collective-permute-start.38 = (bf16[640,896]{1,0:T(8,128)(2,1)S(1)}, bf16[640,896]{1,0:T(8,128)(2,1)S(1)}, u32[]{:S(2)}, u32[]{:S(2)}) collective-permute-start(bf16[640,896]{1,0:T(8,128)(2,1)S(1)} %fusion.19), channel_id=1, source_target_pairs={{0,2},{1,3},{2,0},{3,1},{4,6},{5,7},{6,4},{7,5},{8,10},{9,11},{10,... | collective-permute-start | bytes 3440648 | tf_op jit(solution)/shard_map/ppermute | solution.py:116
  374.4 39.4 %collective-permute-start.25 = (bf16[640,512]{0,1:T(8,128)(2,1)}, bf16[640,512]{0,1:T(8,128)(2,1)}, u32[]{:S(2)}, u32[]{:S(2)}) collective-permute-start(bf16[640,512]{0,1:T(8,128)(2,1)} %convolution_convert_fusion.1), channel_id=1, source_target_pairs={{0,1},{1,0},{2,3},{3,2},{4,5},{5,4},{6,7},{7,6},{8,9},{9,8},{10,11... | collective-permute-start | bytes 1966088 | tf_op jit(solution)/shard_map/ppermute | solution.py:116
  409.2 52.2 %all-to-all-start.4 = ((bf16[4,256,896]{2,1,0:T(8,128)(2,1)}), bf16[4,256,896]{2,1,0:T(8,128)(2,1)}, u32[]{:S(2)}, u32[]{:S(2)}) async-start(bf16[4,256,896]{2,1,0:T(8,128)(2,1)} %bitcast.138), calls=%async_computation.4 | async-start | bytes 3670016 | tf_op jit(solution)/shard_map/all_to_all | solution.py:248
  (102 other events, 1073.8 us)
Sparse Core Ops, SparseCore 0:
  10.1 39.7 all-gather.8
  52.0 35.8 all-gather.14
  89.5 61.9 all-gather.10
  152.9 56.1 all-gather.12
